TPU v7x, 32 devices: a whole 2x2x4 slice. The times are simulated.
32 devices in a mesh: prow: 8 (over z, core), pcol: 4 (over y, x).
Axes of the slice: x: 2, y: 2, z: 4, core: 2. Of those that a mesh axis runs over, the one named last changes fastest.
Arguments:
- right_side: float32 [1024, 4, 4, 1024], P('prow', None, 'pcol'), may hold values from -6 to 6
- inverse_blocks: bfloat16 [2, 1, 8, 1024, 2, 4, 1024], P(None, None, 'prow', None, None, 'pcol'), as said below
- coupling: bfloat16 [1, 8, 1024, 2, 4, 1024], P(None, 'prow', None, None, 'pcol'), may hold values from -0.03125 to 0.03125
- pivots: int32 [2, 8, 1024], P(None, 'prow'), may hold values from 0 to 16383, as said below
Outputs:
- solution: bfloat16 [1024, 2, 8, 1024], P('pcol', None, 'prow')
Inputs may be any that keep to these rules, and one draw needn't show every extreme that they name: `inverse_blocks`: each block is unit upper triangular: ones on its diagonal, zeros below it. Every row number of the window appears exactly once; for every p and p2, exactly 16 * 1024 / 8 ** 2 of the entries pivots[:, p, :] are rows g with (g // 1024) % 8 == p2.
All inputs are finite; a program needn't handle non-finite values.
Results may differ from a plain program's by a relative error of at most 0.0052.
Values may be sent and summed in bfloat16 or wider, within the bound.
A program may use at most 128 MiB of HBM per device.

v0:
```python
import jax
import jax.numpy as jnp
from jax import lax
from jax.sharding import PartitionSpec as P


def body(right_side, inverse_blocks, coupling, pivots):
    rhs_here = right_side.shape[0]
    tiles_across = right_side.shape[1]
    tile_width = right_side.shape[3]
    count_rows = inverse_blocks.shape[1] * tile_width
    count_cols = inverse_blocks.shape[4] * tile_width
    blocks_here = inverse_blocks.shape[1]
    inverse_pair = inverse_blocks.reshape(2, count_rows, count_cols)
    coupling_mat = coupling.reshape(count_rows, count_cols)
    flat_rhs = right_side.reshape(rhs_here, tiles_across * tile_width)
    lower_rhs = flat_rhs[:, :count_cols]
    upper_rhs = flat_rhs[:, count_cols:]
    row_devices = lax.axis_size("prow")
    rhs_total = rhs_here * row_devices
    own_cols = rhs_total // lax.axis_size("pcol")
    contract_last = (((1,), (1,)), ((), ()))

    def solve_with(inverse_mat, portion):
        return lax.dot_general(
            portion, inverse_mat, contract_last, preferred_element_type=jnp.float32
        )

    def as_tiles(solved):
        return solved.reshape(own_cols, blocks_here, 1, tile_width)

    first_partial = solve_with(
        inverse_pair[1], lax.all_gather(upper_rhs.astype(jnp.bfloat16), "prow", axis=0, tiled=True)
    )
    upper_solved = lax.psum_scatter(first_partial, "pcol", scatter_dimension=0, tiled=True).astype(
        jnp.bfloat16
    )
    update_partial = jnp.dot(
        lax.all_gather(upper_solved, "pcol", axis=0, tiled=True),
        coupling_mat,
        preferred_element_type=jnp.float32,
    )
    update = lax.psum_scatter(update_partial, "prow", scatter_dimension=0, tiled=True)
    lower_ready = (lower_rhs - update).astype(jnp.bfloat16)
    second_partial = solve_with(
        inverse_pair[0], lax.all_gather(lower_ready, "prow", axis=0, tiled=True)
    )
    lower_solved = lax.psum_scatter(second_partial, "pcol", scatter_dimension=0, tiled=True).astype(
        jnp.bfloat16
    )
    joined = jnp.concatenate([as_tiles(lower_solved), as_tiles(upper_solved)], axis=1)
    all_rows = lax.all_gather(joined, "prow", axis=2, tiled=True).reshape(own_cols, -1)
    permuted = jnp.take(all_rows, pivots.reshape(-1), axis=1)
    return permuted.reshape(own_cols, pivots.shape[0], 1, tile_width)


def solution(mesh):
    in_specs = (
        P("prow", None, "pcol", None),
        P(None, None, "prow", None, None, "pcol", None),
        P(None, "prow", None, None, "pcol", None),
        P(None, "prow", None),
    )
    out_specs = P("pcol", None, "prow", None)
    return jax.shard_map(body, mesh=mesh, in_specs=in_specs, out_specs=out_specs, check_vma=False)
```

profile of v0, /device:TPU:0, one launch (start us, length us, event | category | flops | bytes accessed | tf_op | source)
XLA Modules:
  0.0 492.8 jit_solution(14746014707884761754)
XLA Ops:
  6.5 7.1 %reduce = f32[128,4,1024]{2,1,0:T(4,128)S(1)} reduce(f32[128,4,1,1024]{3,2,1,0:T(1,128)} %param.4, f32[]{:T(128)} %constant.20), dimensions={2}, to_apply=%param.4.reduce_sub_computation | reduce | bytes 4194308 | tf_op args[0]
  13.6 1.6 copy.9
  15.3 1.3 copy-done
  17.7 7.9 %fusion.1 = (bf16[1,1,1,1024,2,1,1024]{6,4,5,3,2,1,0:T(2,128)(2,1)}, bf16[1,1,1,1024,2,1,1024]{6,4,5,3,2,1,0:T(2,128)(2,1)S(1)}) fusion(bf16[2,1,1,1024,2,1,1024]{6,4,5,3,2,1,0:T(2,128)(2,1)} %param.5), kind=kLoop, calls=%fused_computation.11 | loop fusion | bytes 16777216 | tf_op jit(solution)/shard_map/slice | solution.py:46
  25.7 3.3 copy.10
  29.0 38.2 %all-gather.5.cloned.1.call-done = bf16[1024,2048]{1,0:T(8,128)(2,1)} async-done(((bf16[128,2048]{1,0:T(8,128)(2,1)}), bf16[1024,2048]{1,0:T(8,128)(2,1)}) %all-gather.5.cloned.1.call-update) | async-done | bytes 4194320 | tf_op jit(solution)/shard_map/all_gather | solution.py:33
  67.2 10.0 %fusion.2 = f32[1024,1024]{1,0:T(8,128)} fusion(bf16[1024,2048]{1,0:T(8,128)(2,1)} %all-gather.5.cloned.1.call-done, bf16[1024,2048]{1,0:T(8,128)(2,1)} %bitcast.39), kind=kOutput, calls=%fused_computation.12 | convolution fusion | flops 4294967296 | bytes 12582912 | tf_op jit(solution)/shard_map/dot_general | solution.py:25
  77.3 51.5 %reduce-scatter.4.cloned.1.call-done = f32[256,1024]{1,0:T(8,128)} async-done(((f32[1024,1024]{1,0:T(8,128)}), f32[256,1024]{1,0:T(8,128)}) %reduce-scatter.4.cloned.1.call-update) | async-done | bytes 1048592 | tf_op jit(solution)/shard_map/reduce_scatter | solution.py:35
  128.8 2.1 convert_element_type.10
  131.0 5.5 %copy.11 = bf16[128,8,2,1024]{3,1,2,0:T(8,128)(2,1)} copy(bf16[128,8,2,1024]{3,2,1,0:T(2,128)(2,1)} %bitcast.38) | data formatting | bytes 8388608
  136.5 29.7 %all-gather.7.cloned.1.call-done = bf16[1024,1024]{1,0:T(8,128)(2,1)} async-done(((bf16[256,1024]{1,0:T(8,128)(2,1)}), bf16[1024,1024]{1,0:T(8,128)(2,1)}) %all-gather.7.cloned.1.call-update) | async-done | bytes 2097168 | tf_op jit(solution)/shard_map/all_gather | solution.py:39
  166.3 10.5 %fusion.3 = f32[1024,2048]{1,0:T(8,128)} fusion(bf16[1024,1024]{1,0:T(8,128)(2,1)} %all-gather.7.cloned.1.call-done, bf16[1024,2048]{1,0:T(8,128)(2,1)} %bitcast.41), kind=kOutput, calls=%fused_computation.13 | convolution fusion | flops 4294967296 | bytes 14680064 | tf_op jit(solution)/shard_map/dot_general | solution.py:38
  176.9 89.6 %reduce-scatter.6.cloned.1.call-done = f32[128,2048]{1,0:T(8,128)} async-done(((f32[1024,2048]{1,0:T(8,128)}), f32[128,2048]{1,0:T(8,128)}) %reduce-scatter.6.cloned.1.call-update) | async-done | bytes 1048592 | tf_op jit(solution)/shard_map/reduce_scatter | solution.py:43
  266.5 2.1 fusion
  268.9 5.5 %copy.12 = bf16[128,8,2,1024]{3,1,2,0:T(8,128)(2,1)} copy(bf16[128,8,2,1024]{3,2,1,0:T(2,128)(2,1)} %bitcast.33) | data formatting | bytes 8388608
  274.5 39.7 %all-gather.9.cloned.1.call-done = bf16[1024,2048]{1,0:T(8,128)(2,1)} async-done(((bf16[128,2048]{1,0:T(8,128)(2,1)}), bf16[1024,2048]{1,0:T(8,128)(2,1)}) %all-gather.9.cloned.1.call-update) | async-done | bytes 4194320 | tf_op jit(solution)/shard_map/all_gather | solution.py:46
  314.1 9.9 %fusion.4 = f32[1024,1024]{1,0:T(8,128)} fusion(bf16[1024,2048]{1,0:T(8,128)(2,1)} %all-gather.9.cloned.1.call-done, bf16[1024,2048]{1,0:T(8,128)(2,1)} %bitcast.40), kind=kOutput, calls=%fused_computation.14 | convolution fusion | flops 4294967296 | bytes 12582912 | tf_op jit(solution)/shard_map/dot_general | solution.py:25
  324.2 1.1 copy-done.2
  325.4 50.3 %reduce-scatter.8.cloned.1.call-done = f32[256,1024]{1,0:T(8,128)} async-done(((f32[1024,1024]{1,0:T(8,128)}), f32[256,1024]{1,0:T(8,128)}) %reduce-scatter.8.cloned.1.call-update) | async-done | bytes 1048592 | tf_op jit(solution)/shard_map/reduce_scatter | solution.py:48
  375.7 1.3 convert_bitcast_fusion
  378.1 82.1 %all-gather.11.cloned.1.call-done = bf16[256,2,8,1024]{3,0,2,1:T(8,128)(2,1)} async-done(((bf16[256,2,1,1024]{3,0,2,1:T(8,128)(2,1)}), bf16[256,2,8,1024]{3,0,2,1:T(8,128)(2,1)}) %all-gather.11.cloned.1.call-update) | async-done | bytes 8388624 | tf_op jit(solution)/shard_map/all_gather | solution.py:52
  460.2 11.6 %copy.6 = bf16[256,2,8,1024]{0,3,2,1:T(8,128)(2,1)} copy(bf16[256,2,8,1024]{3,0,2,1:T(8,128)(2,1)} %all-gather.11.cloned.1.call-done) | data formatting | bytes 16777216 | tf_op jit(solution)/shard_map/all_gather | solution.py:52
  471.8 11.1 %gather_fusion = bf16[2048,256]{1,0:T(8,128)(2,1)S(1)} fusion(bf16[256,16384]{0,1:T(8,128)(2,1)} %bitcast.32, s32[2048]{0:T(1024)S(1)} %broadcast_clamp_fusion), kind=kCustom, calls=%fused_computation | custom fusion | bytes 2105344 | tf_op jit(solution)/shard_map/jit(_take)/gather | solution.py:53
  484.1 1.9 broadcast_select_fusion
  (27 shorter events, 3.9 us)
Async XLA Ops:
  6.5 60.7 %all-gather.5.cloned.1.call-start = ((), (), s32[]{:S(2)}) async-start(), calls=%async_computation.3 | async-start | bytes 4718592 | tf_op jit(solution)/shard_map/all_gather | solution.py:33
  15.3 1.3 copy-start
  17.5 111.3 %reduce-scatter.4.cloned.1.call-start = ((), (), s32[]{:S(2)}) async-start(), calls=%async_computation.4 | async-start | bytes 5242880 | tf_op jit(solution)/shard_map/reduce_scatter | solution.py:35
  77.2 89.0 %all-gather.7.cloned.1.call-start = ((), (), s32[]{:S(2)}) async-start(), calls=%async_computation.5 | async-start | bytes 2621440 | tf_op jit(solution)/shard_map/all_gather | solution.py:39
  130.9 135.6 %reduce-scatter.6.cloned.1.call-start = ((), (), s32[]{:S(2)}) async-start(), calls=%async_computation.6 | async-start | bytes 9437184 | tf_op jit(solution)/shard_map/reduce_scatter | solution.py:43
  176.8 89.7 %copy-start.1 = (f32[16,8,4,1024]{3,1,2,0:T(8,128)S(1)}, f32[16,8,4,1024]{3,1,2,0:T(8,128)}, u32[]{:S(2)}) copy-start(f32[16,8,4,1024]{3,1,2,0:T(8,128)} %copy-done) | copy-start | bytes 6291460
  176.8 137.3 %all-gather.9.cloned.1.call-start = ((), (), s32[]{:S(2)}) async-start(), calls=%async_computation.7 | async-start | bytes 4718592 | tf_op jit(solution)/shard_map/all_gather | solution.py:46
  268.7 107.0 %reduce-scatter.8.cloned.1.call-start = ((), (), s32[]{:S(2)}) async-start(), calls=%async_computation.8 | async-start | bytes 5242880 | tf_op jit(solution)/shard_map/reduce_scatter | solution.py:48
  324.1 1.2 copy-start.2
  324.1 53.9 %copy-start.3 = (s32[2,1,1024]{2,1,0:T(1,128)S(1)}, s32[2,1,1024]{2,1,0:T(1,128)}, u32[]{:S(2)}) copy-start(s32[2,1,1024]{2,1,0:T(1,128)} %param.7) | copy-start | bytes 24580
  324.1 136.1 %all-gather.11.cloned.1.call-start = ((), (), s32[]{:S(2)}) async-start(), calls=%async_computation.9 | async-start | bytes 9437184 | tf_op jit(solution)/shard_map/all_gather | solution.py:52
Sparse Core Ops, SparseCore 0:
  17.6 49.5 all-gather.4
  77.4 51.3 reduce-scatter.3
  131.0 35.1 all-gather.6
  176.9 89.5 reduce-scatter.5
  268.8 45.3 all-gather.8
  324.2 51.3 reduce-scatter.7
  378.2 82.0 all-gather.10
where the time goes:
time: 494 us; the launch traced here: 493 us
  waiting for transfers between devices  381 us (77%)
  local copies, waits for them, and re-layouts  51.2 us (10%)
  matrix products  30.4 us (6%)
  other arithmetic  15.6 us (3%)
  between operations  13.6 us (3%)
    reduce_scatter x1, waiting for transfers between devices, body(): lax.psum_scatter(update_partial, 'prow', scatter_dimension=0, tiled=True)  89.6 us
    all_gather x1, waiting for transfers between devices, body(): lax.all_gather(joined, 'prow', axis=2, tiled=True).reshape(own_cols, -1)  82.1 us
    reduce_scatter x1, waiting for transfers between devices, body(): lax.psum_scatter(first_partial, 'pcol', scatter_dimension=0, tiled=True)  51.5 us
    reduce_scatter x1, waiting for transfers between devices, body(): lax.psum_scatter(second_partial, 'pcol', scatter_dimension=0, tiled=True)  50.3 us
    all_gather x1, waiting for transfers between devices, body(): lax.all_gather(lower_ready, 'prow', axis=0, tiled=True)  39.7 us
    all_gather x1, waiting for transfers between devices, body(): lax.all_gather(upper_rhs.astype(jnp.bfloat16), 'prow', axis=0, tiled=True)  38.2 us
    all_gather x1, waiting for transfers between devices, body(): lax.all_gather(upper_solved, 'pcol', axis=0, tiled=True)  29.7 us
    dot_general x2, matrix products, solve_with(): lax.dot_general(portion, inverse_mat, contract_last, preferred_element_ty...  19.9 us
  transfers between devices with their start and end apart: 7, of which 7 were waited for; matrix products, arithmetic and copies ran while one was open for 5% of the time, Pallas kernels for 0%

commit v1 on v0

--- a/solution.py
+++ b/solution.py
@@ -2,6 +2,28 @@
 import jax.numpy as jnp
 from jax import lax
 from jax.sharding import PartitionSpec as P
+
+
+def laid_out(parts, dim):
+    parts = jnp.moveaxis(parts, 0, dim)
+    shape = parts.shape
+    return parts.reshape(*shape[:dim], shape[dim] * shape[dim + 1], *shape[dim + 2 :])
+
+
+def gather_around(x, axis, dim):
+    count = lax.axis_size(axis)
+    pairs = [(i, (i + 1) % count) for i in range(count)]
+    back = [(b, a) for a, b in pairs]
+    lower, upper = ([], [])
+    for step in range(count - 1):
+        if step % 2 == 0:
+            lower.append(lax.ppermute(lower[-1] if lower else x, axis, pairs))
+        else:
+            upper.append(lax.ppermute(upper[-1] if upper else x, axis, back))
+    pieces = jnp.stack([*lower[::-1], x, *upper])
+    shift = lax.axis_index(axis) - len(lower)
+    pieces = pieces[(jnp.arange(count) - shift) % count]
+    return laid_out(pieces, dim)
 
 
 def body(right_side, inverse_blocks, coupling, pivots):
@@ -49,7 +71,7 @@
         jnp.bfloat16
     )
     joined = jnp.concatenate([as_tiles(lower_solved), as_tiles(upper_solved)], axis=1)
-    all_rows = lax.all_gather(joined, "prow", axis=2, tiled=True).reshape(own_cols, -1)
+    all_rows = gather_around(joined, "prow", 2).reshape(own_cols, -1)
     permuted = jnp.take(all_rows, pivots.reshape(-1), axis=1)
     return permuted.reshape(own_cols, pivots.shape[0], 1, tile_width)
 

time: 494 us -> 525 us (1.063)
  local copies, waits for them, and re-layouts: 51.2 us -> 70.6 us
  starting transfers between devices: 0.65 us -> 11.4 us
    ppermute x0 -> x7, waiting for transfers between devices: none -> 82.8 us  [the longest x4 82.8 us: gather_around(): lower.append(lax.ppermute(lower[-1] if lower else x, axis, pairs))]
    all_gather x1 -> x0, waiting for transfers between devices: 82.1 us -> none  [body(): lax.all_gather(joined, 'prow', axis=2, tiled=True).reshape(own_cols, -1)]
    transpose x0 -> x1, local copies, waits for them, and re-layouts: none -> 11.9 us  [laid_out(): parts = jnp.moveaxis(parts, 0, dim)]
    all_gather x1 -> x0, local copies, waits for them, and re-layouts: 11.6 us -> none  [body(): lax.all_gather(joined, 'prow', axis=2, tiled=True).reshape(own_cols, -1)]
    ppermute x0 -> x7, starting transfers between devices: none -> 10.7 us  [the longest x3 10.7 us: gather_around(): upper.append(lax.ppermute(upper[-1] if upper else x, axis, back))]
    unnamed x12 -> x18, local copies, waits for them, and re-layouts: 18.6 us -> 28.6 us
    gather x0 -> x1, local copies, waits for them, and re-layouts: none -> 8.07 us  [gather_around(): pieces = pieces[(jnp.arange(count) - shift) % count]]
  transfers between devices with their start and end apart: 7 -> 13, of which waited for: 7 -> 10; matrix products, arithmetic and copies ran while one was open for 5% -> 6% of each run, Pallas kernels for 0% -> 0%
where the time goes in v1:
time: 525 us; the launch traced here: 524 us
  waiting for transfers between devices  382 us (73%)
  local copies, waits for them, and re-layouts  70.6 us (13%)
  matrix products  30.5 us (6%)
  other arithmetic  15.8 us (3%)
  between operations  13.6 us (3%)
  starting transfers between devices  11.4 us (2%)
    reduce_scatter x1, waiting for transfers between devices, body(): lax.psum_scatter(update_partial, 'prow', scatter_dimension=0, tiled=True)  89.6 us
    ppermute x4, waiting for transfers between devices, gather_around(): lower.append(lax.ppermute(lower[-1] if lower else x, axis, pairs))  82.8 us
    reduce_scatter x1, waiting for transfers between devices, body(): lax.psum_scatter(first_partial, 'pcol', scatter_dimension=0, tiled=True)  51.5 us
    reduce_scatter x1, waiting for transfers between devices, body(): lax.psum_scatter(second_partial, 'pcol', scatter_dimension=0, tiled=True)  50.3 us
    all_gather x1, waiting for transfers between devices, body(): lax.all_gather(lower_ready, 'prow', axis=0, tiled=True)  39.7 us
    all_gather x1, waiting for transfers between devices, body(): lax.all_gather(upper_rhs.astype(jnp.bfloat16), 'prow', axis=0, tiled=True)  38.2 us
    all_gather x1, waiting for transfers between devices, body(): lax.all_gather(upper_solved, 'pcol', axis=0, tiled=True)  29.8 us
    unnamed x18, local copies, waits for them, and re-layouts  28.6 us
  transfers between devices with their start and end apart: 13, of which 10 were waited for; matrix products, arithmetic and copies ran while one was open for 6% of the time, Pallas kernels for 0%

profile of v1, /device:TPU:0, one launch (start us, length us, event | category | flops | bytes accessed | tf_op | source)
XLA Modules:
  0.0 523.8 jit_solution(15859851625660539404)
XLA Ops:
  6.5 7.1 %reduce = f32[128,4,1024]{2,1,0:T(4,128)S(1)} reduce(f32[128,4,1,1024]{3,2,1,0:T(1,128)} %param.4, f32[]{:T(128)} %constant.45), dimensions={2}, to_apply=%param.4.reduce_sub_computation | reduce | bytes 4194308 | tf_op args[0]
  17.7 7.9 %fusion.4 = (bf16[1,1,1,1024,2,1,1024]{6,4,5,3,2,1,0:T(2,128)(2,1)}, bf16[1,1,1,1024,2,1,1024]{6,4,5,3,2,1,0:T(2,128)(2,1)S(1)}) fusion(bf16[2,1,1,1024,2,1,1024]{6,4,5,3,2,1,0:T(2,128)(2,1)} %param.5), kind=kLoop, calls=%fused_computation.28 | loop fusion | bytes 16777216 | tf_op jit(solution)/shard_map/slice | solution.py:68
  25.7 3.3 copy.12
  29.0 38.2 %all-gather.4.cloned.1.call-done = bf16[1024,2048]{1,0:T(8,128)(2,1)} async-done(((bf16[128,2048]{1,0:T(8,128)(2,1)}), bf16[1024,2048]{1,0:T(8,128)(2,1)}) %all-gather.4.cloned.1.call-update) | async-done | bytes 4194320 | tf_op jit(solution)/shard_map/all_gather | solution.py:55
  67.3 10.0 %fusion.5 = f32[1024,1024]{1,0:T(8,128)} fusion(bf16[1024,2048]{1,0:T(8,128)(2,1)} %all-gather.4.cloned.1.call-done, bf16[1024,2048]{1,0:T(8,128)(2,1)} %bitcast.64), kind=kOutput, calls=%fused_computation.29 | convolution fusion | flops 4294967296 | bytes 12582912 | tf_op jit(solution)/shard_map/dot_general | solution.py:47
  77.3 51.5 %reduce-scatter.4.cloned.1.call-done = f32[256,1024]{1,0:T(8,128)} async-done(((f32[1024,1024]{1,0:T(8,128)}), f32[256,1024]{1,0:T(8,128)}) %reduce-scatter.4.cloned.1.call-update) | async-done | bytes 1048592 | tf_op jit(solution)/shard_map/reduce_scatter | solution.py:57
  131.0 5.5 %copy.13 = bf16[128,8,2,1024]{3,1,2,0:T(8,128)(2,1)} copy(bf16[128,8,2,1024]{3,2,1,0:T(2,128)(2,1)} %bitcast.63) | data formatting | bytes 8388608
  136.5 29.8 %all-gather.6.cloned.1.call-done = bf16[1024,1024]{1,0:T(8,128)(2,1)} async-done(((bf16[256,1024]{1,0:T(8,128)(2,1)}), bf16[1024,1024]{1,0:T(8,128)(2,1)}) %all-gather.6.cloned.1.call-update) | async-done | bytes 2097168 | tf_op jit(solution)/shard_map/all_gather | solution.py:61
  166.3 10.6 %fusion.6 = f32[1024,2048]{1,0:T(8,128)} fusion(bf16[1024,1024]{1,0:T(8,128)(2,1)} %all-gather.6.cloned.1.call-done, bf16[1024,2048]{1,0:T(8,128)(2,1)} %bitcast.66), kind=kOutput, calls=%fused_computation.30 | convolution fusion | flops 4294967296 | bytes 14680064 | tf_op jit(solution)/shard_map/dot_general | solution.py:60
  176.9 89.6 %reduce-scatter.6.cloned.1.call-done = f32[128,2048]{1,0:T(8,128)} async-done(((f32[1024,2048]{1,0:T(8,128)}), f32[128,2048]{1,0:T(8,128)}) %reduce-scatter.6.cloned.1.call-update) | async-done | bytes 1048592 | tf_op jit(solution)/shard_map/reduce_scatter | solution.py:65
  269.0 5.5 %copy.14 = bf16[128,8,2,1024]{3,1,2,0:T(8,128)(2,1)} copy(bf16[128,8,2,1024]{3,2,1,0:T(2,128)(2,1)} %bitcast.58) | data formatting | bytes 8388608
  274.5 39.7 %all-gather.8.cloned.1.call-done = bf16[1024,2048]{1,0:T(8,128)(2,1)} async-done(((bf16[128,2048]{1,0:T(8,128)(2,1)}), bf16[1024,2048]{1,0:T(8,128)(2,1)}) %all-gather.8.cloned.1.call-update) | async-done | bytes 4194320 | tf_op jit(solution)/shard_map/all_gather | solution.py:68
  314.2 9.9 %fusion.7 = f32[1024,1024]{1,0:T(8,128)} fusion(bf16[1024,2048]{1,0:T(8,128)(2,1)} %all-gather.8.cloned.1.call-done, bf16[1024,2048]{1,0:T(8,128)(2,1)} %bitcast.65), kind=kOutput, calls=%fused_computation.31 | convolution fusion | flops 4294967296 | bytes 12582912 | tf_op jit(solution)/shard_map/dot_general | solution.py:47
  325.4 50.3 %reduce-scatter.8.cloned.1.call-done = f32[256,1024]{1,0:T(8,128)} async-done(((f32[1024,1024]{1,0:T(8,128)}), f32[256,1024]{1,0:T(8,128)}) %reduce-scatter.8.cloned.1.call-update) | async-done | bytes 1048592 | tf_op jit(solution)/shard_map/reduce_scatter | solution.py:70
  377.2 16.0 %collective-permute-done = bf16[256,2,1,1024]{3,0,1,2:T(8,128)(2,1)S(1)} collective-permute-done((bf16[256,2,1,1024]{3,0,1,2:T(8,128)(2,1)S(1)}, bf16[256,2,1,1024]{3,0,1,2:T(8,128)(2,1)S(1)}, u32[]{:S(2)}, u32[]{:S(2)}) %collective-permute-start) | collective-permute-done | bytes 1048608 | tf_op jit(solution)/shard_map/ppermute | solution.py:20
  393.2 3.5 collective-permute-start.4
  396.8 23.8 %collective-permute-done.1 = bf16[256,2,1,1024]{3,0,1,2:T(8,128)(2,1)} collective-permute-done((bf16[256,2,1,1024]{3,0,1,2:T(8,128)(2,1)S(1)}, bf16[256,2,1,1024]{3,0,1,2:T(8,128)(2,1)}, u32[]{:S(2)}, u32[]{:S(2)}) %collective-permute-start.1) | collective-permute-done | bytes 1048608 | tf_op jit(solution)/shard_map/ppermute | solution.py:20
  420.6 3.5 collective-permute-start.5
  424.1 22.6 %collective-permute-done.2 = bf16[256,2,1,1024]{3,0,1,2:T(8,128)(2,1)} collective-permute-done((bf16[256,2,1,1024]{3,0,1,2:T(8,128)(2,1)}, bf16[256,2,1,1024]{3,0,1,2:T(8,128)(2,1)}, u32[]{:S(2)}, u32[]{:S(2)}) %collective-permute-start.2) | collective-permute-done | bytes 1048608 | tf_op jit(solution)/shard_map/ppermute | solution.py:20
  446.8 3.6 collective-permute-start.6
  450.4 20.4 %collective-permute-done.3 = bf16[256,2,1,1024]{3,0,1,2:T(8,128)(2,1)S(1)} collective-permute-done((bf16[256,2,1,1024]{3,0,1,2:T(8,128)(2,1)}, bf16[256,2,1,1024]{3,0,1,2:T(8,128)(2,1)S(1)}, u32[]{:S(2)}, u32[]{:S(2)}) %collective-permute-start.3) | collective-permute-done | bytes 1048608 | tf_op jit(solution)/shard_map/ppermute | solution.py:20
  483.0 8.1 %gather_fusion = bf16[8,256,2,1024]{3,1,2,0:T(8,128)(2,1)} fusion(bf16[8,256,2,1024]{3,1,2,0:T(8,128)(2,1)} %bitcast.11, s32[1024]{0:T(1024)S(1)} %pad_clamp_fusion), kind=kCustom, calls=%fused_computation | custom fusion | bytes 16777248 | tf_op jit(solution)/shard_map/gather | solution.py:25
  491.0 11.9 %copy.8 = bf16[256,2,8,1,1024]{0,4,2,1,3:T(8,128)(2,1)} copy(bf16[256,2,8,1,1024]{4,0,1,2,3:T(8,128)(2,1)} %bitcast.56) | data formatting | bytes 16777216 | tf_op jit(solution)/shard_map/transpose | solution.py:8
  502.9 11.1 %gather_fusion.1 = bf16[2048,256]{1,0:T(8,128)(2,1)S(1)} fusion(bf16[256,16384]{0,1:T(8,128)(2,1)} %bitcast.57, s32[2048]{0:T(1024)S(1)} %broadcast_clamp_fusion), kind=kCustom, calls=%fused_computation.1 | custom fusion | bytes 2105344 | tf_op jit(solution)/shard_map/jit(_take)/gather | solution.py:75
  (49 shorter events, 26.7 us)
Async XLA Ops:
  6.5 60.7 %all-gather.4.cloned.1.call-start = ((), (), s32[]{:S(2)}) async-start(), calls=%async_computation.3 | async-start | bytes 4718592 | tf_op jit(solution)/shard_map/all_gather | solution.py:55
  15.3 1.3 copy-start
  17.5 111.3 %reduce-scatter.4.cloned.1.call-start = ((), (), s32[]{:S(2)}) async-start(), calls=%async_computation.4 | async-start | bytes 5242880 | tf_op jit(solution)/shard_map/reduce_scatter | solution.py:57
  77.2 89.0 %all-gather.6.cloned.1.call-start = ((), (), s32[]{:S(2)}) async-start(), calls=%async_computation.5 | async-start | bytes 2621440 | tf_op jit(solution)/shard_map/all_gather | solution.py:61
  130.9 135.6 %reduce-scatter.6.cloned.1.call-start = ((), (), s32[]{:S(2)}) async-start(), calls=%async_computation.6 | async-start | bytes 9437184 | tf_op jit(solution)/shard_map/reduce_scatter | solution.py:65
  176.8 89.7 %copy-start.1 = (f32[16,8,4,1024]{3,1,2,0:T(8,128)S(1)}, f32[16,8,4,1024]{3,1,2,0:T(8,128)}, u32[]{:S(2)}) copy-start(f32[16,8,4,1024]{3,1,2,0:T(8,128)} %copy-done) | copy-start | bytes 6291460
  176.9 137.3 %all-gather.8.cloned.1.call-start = ((), (), s32[]{:S(2)}) async-start(), calls=%async_computation.7 | async-start | bytes 4718592 | tf_op jit(solution)/shard_map/all_gather | solution.py:68
  268.7 107.0 %reduce-scatter.8.cloned.1.call-start = ((), (), s32[]{:S(2)}) async-start(), calls=%async_computation.8 | async-start | bytes 5242880 | tf_op jit(solution)/shard_map/reduce_scatter | solution.py:70
  324.1 1.2 copy-start.2
  325.3 121.4 %copy-start.3 = (s32[2,1,1024]{2,1,0:T(1,128)S(1)}, s32[2,1,1024]{2,1,0:T(1,128)}, u32[]{:S(2)}) copy-start(s32[2,1,1024]{2,1,0:T(1,128)} %param.7) | copy-start | bytes 24580
  377.1 16.1 %collective-permute-start = (bf16[256,2,1,1024]{3,0,1,2:T(8,128)(2,1)S(1)}, bf16[256,2,1,1024]{3,0,1,2:T(8,128)(2,1)S(1)}, u32[]{:S(2)}, u32[]{:S(2)}) collective-permute-start(bf16[256,2,1,1024]{3,0,1,2:T(8,128)(2,1)S(1)} %get-tuple-element.8), channel_id=1, source_target_pairs={{0,4},{4,8},{8,12},{12,16},{16,20},{20,24},{24,28},{28,0},{1,5},{5... | collective-permute-start | bytes 3145736 | tf_op jit(solution)/shard_map/ppermute | solution.py:20
  393.2 27.3 %collective-permute-start.1 = (bf16[256,2,1,1024]{3,0,1,2:T(8,128)(2,1)S(1)}, bf16[256,2,1,1024]{3,0,1,2:T(8,128)(2,1)}, u32[]{:S(2)}, u32[]{:S(2)}) collective-permute-start(bf16[256,2,1,1024]{3,0,1,2:T(8,128)(2,1)S(1)} %collective-permute-done), channel_id=1, source_target_pairs={{0,4},{4,8},{8,12},{12,16},{16,20},{20,24},{24,28},{28,0},{1,5},{5... | collective-permute-start | bytes 3145736 | tf_op jit(solution)/shard_map/ppermute | solution.py:20
  393.2 27.3 %collective-permute-start.4 = (bf16[256,2,1,1024]{3,0,2,1:T(8,128)(2,1)S(1)}, bf16[256,2,1,1024]{3,0,2,1:T(8,128)(2,1)}, u32[]{:S(2)}, u32[]{:S(2)}) collective-permute-start(bf16[256,2,1,1024]{3,0,2,1:T(8,128)(2,1)S(1)} %get-tuple-element.7), channel_id=1, source_target_pairs={{4,0},{8,4},{12,8},{16,12},{20,16},{24,20},{28,24},{0,28},{5,1},{9... | collective-permute-start | bytes 3145736 | tf_op jit(solution)/shard_map/ppermute | solution.py:22
  420.6 26.2 %collective-permute-start.2 = (bf16[256,2,1,1024]{3,0,1,2:T(8,128)(2,1)}, bf16[256,2,1,1024]{3,0,1,2:T(8,128)(2,1)}, u32[]{:S(2)}, u32[]{:S(2)}) collective-permute-start(bf16[256,2,1,1024]{3,0,1,2:T(8,128)(2,1)} %collective-permute-done.1), channel_id=1, source_target_pairs={{0,4},{4,8},{8,12},{12,16},{16,20},{20,24},{24,28},{28,0},{1,5},{5... | collective-permute-start | bytes 3145736 | tf_op jit(solution)/shard_map/ppermute | solution.py:20
  420.6 26.3 %collective-permute-start.5 = (bf16[256,2,1,1024]{3,0,2,1:T(8,128)(2,1)}, bf16[256,2,1,1024]{3,0,2,1:T(8,128)(2,1)S(1)}, u32[]{:S(2)}, u32[]{:S(2)}) collective-permute-start(bf16[256,2,1,1024]{3,0,2,1:T(8,128)(2,1)} %collective-permute-done.4), channel_id=1, source_target_pairs={{4,0},{8,4},{12,8},{16,12},{20,16},{24,20},{28,24},{0,28},{5,1},{9... | collective-permute-start | bytes 3145736 | tf_op jit(solution)/shard_map/ppermute | solution.py:22
  446.7 24.1 %collective-permute-start.3 = (bf16[256,2,1,1024]{3,0,1,2:T(8,128)(2,1)}, bf16[256,2,1,1024]{3,0,1,2:T(8,128)(2,1)S(1)}, u32[]{:S(2)}, u32[]{:S(2)}) collective-permute-start(bf16[256,2,1,1024]{3,0,1,2:T(8,128)(2,1)} %collective-permute-done.2), channel_id=1, source_target_pairs={{0,4},{4,8},{8,12},{12,16},{16,20},{20,24},{24,28},{28,0},{1,5},{5... | collective-permute-start | bytes 3145736 | tf_op jit(solution)/shard_map/ppermute | solution.py:20
  446.8 35.0 %collective-permute-start.6 = (bf16[256,2,1,1024]{3,0,2,1:T(8,128)(2,1)S(1)}, bf16[256,2,1,1024]{3,0,2,1:T(8,128)(2,1)S(1)}, u32[]{:S(2)}, u32[]{:S(2)}) collective-permute-start(bf16[256,2,1,1024]{3,0,2,1:T(8,128)(2,1)S(1)} %collective-permute-done.5), channel_id=1, source_target_pairs={{4,0},{8,4},{12,8},{16,12},{20,16},{24,20},{28,24},{0,28},{5,1},{9... | collective-permute-start | bytes 3145736 | tf_op jit(solution)/shard_map/ppermute | solution.py:22
Sparse Core Ops, SparseCore 0:
  17.6 49.5 all-gather.3
  77.4 51.3 reduce-scatter.3
  131.0 35.1 all-gather.5
  177.0 89.5 reduce-scatter.5
  268.8 45.3 all-gather.7
  324.2 51.3 reduce-scatter.7
